TPU v7x, 32 devices: a whole 2x2x4 slice. The times are simulated.
32 devices in a mesh: grp: 2 (over x), sub: 16 (over z, y, core).
Axes of the slice: x: 2, y: 2, z: 4, core: 2. Of those that a mesh axis runs over, the one named last changes fastest.
Arguments:
- resid: bfloat16 [2, 32, 2, 512, 256], P('grp', 'sub'), may hold values from -6 to 6
- kinv: bfloat16 [2, 32, 2, 512, 512], P('grp', 'sub'), may hold values from -2 to 2
- basis: bfloat16 [2, 32, 2, 8, 512], P('grp', 'sub'), may hold values from -2 to 2
- counts: int32 [2, 32], P('grp', 'sub'), may hold values from 1 to 8, as said below
- coarse_map: int32 [2, 32, 8], P('grp', 'sub'), may hold values from 0 to 127, as said below
- coarse_inv: float32 [2, 2, 128, 128], P('grp', None, 'sub'), may hold values from -1 to 1
Outputs:
- correction: bfloat16 [2, 32, 2, 512, 256], P('grp', 'sub')
Inputs may be any that keep to these rules, and one draw needn't show every extreme that they name: `counts`: every draw has a subdomain with 8 live constraints. `coarse_map`: the constraints of subdomain j name coarse unknowns from 4 * j - 4 to 4 * j + 2 * 4 - 1, modulo 128; slots past the count hold values too.
All inputs are finite; a program needn't handle non-finite values.
Results may differ from a plain program's by a relative error of at most 0.0034.
Values may be sent and summed in bfloat16 or wider, within the bound.
A program may use at most 64 MiB of HBM per device.

v0:
```python
import jax
import jax.numpy as jnp
from jax import lax
from jax.sharding import PartitionSpec as P

IF = 64
PMAX = 8
CPS = 4


def shifted(value, axis, steps):
    count = lax.axis_size(axis)
    pairs = [(source, (source + steps) % count) for source in range(count)]
    return lax.ppermute(value, axis, pairs)


def shifted_2(block, axis, distance):
    devices = range(lax.axis_size(axis))
    route = [(i - distance, i) for i in devices if i - distance in devices]
    return lax.ppermute(block, axis, route)


def product_low(matrix, vector):
    parts = jnp.einsum("scik,sdkr->scdir", matrix, vector, preferred_element_type=jnp.float32)
    return jnp.stack([parts[:, 0, 0] - parts[:, 1, 1], parts[:, 0, 1] + parts[:, 1, 0]], axis=1)


def product_high(matrix, vector):
    parts = jnp.einsum("...cik,...dkr->...cdir", matrix, vector, precision=lax.Precision.HIGHEST)
    real_part = parts[..., 0, 0, :, :] - parts[..., 1, 1, :, :]
    imag_part = parts[..., 0, 1, :, :] + parts[..., 1, 0, :, :]
    return jnp.stack([real_part, imag_part], axis=-3)


def coarse_rows_product(coarse, rhs_rows):
    parts = jnp.einsum("aik,kbr->abir", coarse, rhs_rows, precision=lax.Precision.HIGHEST)
    return jnp.stack([parts[0, 0] - parts[1, 1], parts[0, 1] + parts[1, 0]], axis=1)


def window_table(mapped, first_sub, order_coarse):
    global_ids = first_sub + lax.broadcasted_iota(jnp.int32, mapped.shape, 0)
    relative = jnp.mod(mapped - CPS * global_ids + CPS, order_coarse)
    spots = lax.broadcasted_iota(jnp.int32, (1, 1, 3 * CPS), 2)
    return (relative[:, :, None] == spots).astype(jnp.float32)


def window_terms(onehot, primal):
    subs = primal.shape[0]
    terms = jnp.einsum("spw,scpr->swcr", onehot, primal, precision=lax.Precision.HIGHEST)
    return terms.reshape(subs, 3, CPS, 2, primal.shape[3])


def cyclic_blocks(terms):
    return jnp.roll(terms[:, 0], -1, axis=0) + terms[:, 1] + jnp.roll(terms[:, 2], 1, axis=0)


def per_device(resid, kinv, basis, counts, coarse_map, coarse_inv):
    values = resid[0]
    inverses = kinv[0]
    shapes = basis[0]
    counted = counts[0]
    mapped = coarse_map[0]
    coarse = coarse_inv[0]
    subs = values.shape[0]
    width_rhs = values.shape[3]
    order_coarse = coarse.shape[2]
    first_sub = lax.axis_index("sub") * subs
    lefts = values[:, :, :IF]
    rights = values[:, :, IF : 2 * IF]
    lowers = values[:, :, 2 * IF : 3 * IF]
    uppers = values[:, :, 3 * IF : 4 * IF]
    from_prev = shifted(rights[subs - 1 :], "sub", 1)
    from_next = shifted(lefts[:1], "sub", -1)
    from_below = shifted_2(uppers, "grp", 1)
    from_above = shifted_2(lowers, "grp", -1)
    group = lax.axis_index("grp")
    groups = lax.axis_size("grp")
    low_weight = jnp.where(group > 0, 0.5, 1.0).astype(jnp.float32)
    high_weight = jnp.where(group < groups - 1, 0.5, 1.0).astype(jnp.float32)
    beside = jnp.concatenate(
        [
            jnp.concatenate([from_prev, rights[: subs - 1]], axis=0),
            jnp.concatenate([lefts[1:], from_next], axis=0),
            from_below,
            from_above,
        ],
        axis=2,
    ).astype(jnp.float32)
    shared = (
        jnp.concatenate(
            [
                0.5 * lefts.astype(jnp.float32),
                0.5 * rights.astype(jnp.float32),
                low_weight * lowers.astype(jnp.float32),
                high_weight * uppers.astype(jnp.float32),
            ],
            axis=2,
        )
        + 0.5 * beside
    )
    weighted = jnp.concatenate([shared.astype(jnp.bfloat16), values[:, :, 4 * IF :]], axis=2)
    local = product_low(inverses, weighted)
    primal = product_low(shapes, weighted)
    slots = lax.broadcasted_iota(jnp.int32, (subs, PMAX), 1)
    live = (slots < counted[:, None]).astype(jnp.float32)
    primal = primal * live[:, None, :, None]
    onehot = window_table(mapped, first_sub, order_coarse) * live[:, :, None]
    all_primal, all_map = (
        lax.all_gather(primal, "sub", axis=0, tiled=True),
        lax.all_gather(mapped, "sub", axis=0, tiled=True),
    )
    all_onehot = window_table(all_map, 0, order_coarse)
    rhs = cyclic_blocks(window_terms(all_onehot, all_primal)).reshape(order_coarse, 2, width_rhs)
    solved = coarse_rows_product(coarse, rhs)
    before = shifted(solved[solved.shape[0] - CPS :], "sub", 1)
    after = shifted(solved[:CPS], "sub", -1)
    window = jnp.concatenate([before, solved, after], axis=0)
    windows = jnp.stack([window[CPS * s : CPS * s + 3 * CPS] for s in range(subs)], axis=0)
    picked = jnp.einsum("spw,swcr->scpr", onehot, windows, precision=lax.Precision.HIGHEST)
    spread = product_high(jnp.swapaxes(shapes, 2, 3).astype(jnp.float32), picked)
    return (local + spread).astype(jnp.bfloat16)[None]


def solution(mesh):
    return jax.shard_map(
        per_device,
        mesh=mesh,
        in_specs=(
            P("grp", "sub", None, None, None),
            P("grp", "sub", None, None, None),
            P("grp", "sub", None, None, None),
            P("grp", "sub"),
            P("grp", "sub", None),
            P("grp", None, "sub", None),
        ),
        out_specs=P("grp", "sub", None, None, None),
        check_vma=False,
    )
```

profile of v0, /device:TPU:31, one launch (start us, length us, event | category | flops | bytes accessed | tf_op | source)
XLA Modules:
  0.0 70.1 jit_solution(6519834105056255239)
XLA Ops:
  0.0 1.6 %copy.49 = bf16[1,2,2,512,256]{3,4,2,1,0:T(8,128)(2,1)S(1)} copy(bf16[1,2,2,512,256]{4,3,2,1,0:T(8,128)(2,1)} %param.6) | data formatting | bytes 2097152 | tf_op args[0]
  1.6 0.8 %fusion.42 = (bf16[1,2,64,256]{2,3,1,0:T(8,128)(2,1)}, bf16[1,2,64,256]{2,3,1,0:T(8,128)(2,1)}, bf16[1,2,64,256]{2,3,1,0:T(8,128)(2,1)S(1)}, bf16[1,2,64,256]{2,3,1,0:T(8,128)(2,1)S(1)}) fusion(bf16[2,2,512,256]{2,3,1,0:T(8,128)(2,1)S(1)} %bitcast.132), kind=kLoop, calls=%fused_computation.87 | loop fusion | bytes 524288 | tf_op jit(solution)/shard_map/slice | solution.py:72
  2.5 0.4 collective-permute-start
  2.9 0.2 collective-permute-start.1
  3.1 0.9 %fusion.43 = (bf16[2,2,64,256]{2,3,1,0:T(8,128)(2,1)}, bf16[2,2,64,256]{2,3,1,0:T(8,128)(2,1)}) fusion(bf16[2,2,512,256]{2,3,1,0:T(8,128)(2,1)S(1)} %bitcast.133), kind=kLoop, calls=%fused_computation.88 | loop fusion | bytes 524288 | tf_op jit(solution)/shard_map/slice | solution.py:71
  4.0 1.3 %collective-permute-start.2 = (bf16[2,2,64,256]{2,3,1,0:T(8,128)(2,1)}, bf16[2,2,64,256]{2,3,1,0:T(8,128)(2,1)}, u32[]{:S(2)}, u32[]{:S(2)}) collective-permute-start(bf16[2,2,64,256]{2,3,1,0:T(8,128)(2,1)} %get-tuple-element.11), channel_id=1, source_target_pairs={{0,16},{1,17},{2,18},{3,19},{4,20},{5,21},{6,22},{7,23},{8,24},{9,... | collective-permute-start | bytes 393224 | tf_op jit(solution)/shard_map/ppermute | solution.py:20
  5.3 5.4 %collective-permute-start.3 = (bf16[2,2,64,256]{2,3,1,0:T(8,128)(2,1)}, bf16[2,2,64,256]{2,3,1,0:T(8,128)(2,1)}, u32[]{:S(2)}, u32[]{:S(2)}) collective-permute-start(bf16[2,2,64,256]{2,3,1,0:T(8,128)(2,1)} %get-tuple-element.12), channel_id=1, source_target_pairs={{16,0},{17,1},{18,2},{19,3},{20,4},{21,5},{22,6},{23,7},{24,8},{25... | collective-permute-start | bytes 393224 | tf_op jit(solution)/shard_map/ppermute | solution.py:20
  10.7 0.6 iota_multiply_fusion
  11.3 19.6 %all-gather = s32[1,32,8]{2,0,1:T(1,128)S(1)} all-gather(s32[1,2,8]{2,0,1:T(1,128)} %bitcast.141), channel_id=2, replica_groups=mesh['grp'=2,'sub'=16] {'sub'}, dimensions={1}, use_global_device_ids=true | all-gather | bytes 1088 | tf_op jit(solution)/shard_map/all_gather | solution.py:110
  30.9 0.8 %and_select_fusion = s32[2,8]{1,0:T(2,128)S(1)} fusion(s32[1,2,8]{2,1,0:T(2,128)} %param.10, s32[2]{0:T(128)S(1)} %add_multiply_fusion), kind=kLoop, calls=%fused_computation.76 | loop fusion | flops 208 | bytes 136 | tf_op jit(solution)/shard_map/jit(remainder)/select_n | solution.py:42
  31.7 0.2 convert_multiply_fusion.3
  32.2 1.8 %fusion.7 = bf16[2,2,256,256]{2,3,1,0:T(8,128)(2,1)S(1)} fusion(f32[2,2,64,256]{2,3,1,0:T(8,128)S(1)} %get-tuple-element.15, f32[2,2,64,256]{2,3,1,0:T(8,128)S(1)} %get-tuple-element.14, f32[2,2,64,256]{2,3,1,0:T(8,128)S(1)} %get-tuple-element.16, f32[2,2,64,256]{2,3,1,0:T(8,128)S(1)} %get-tuple-element.13, ...), kind=kLoop, calls=%fused_computation.19 | loop fusion | flops 4718592 | bytes 2097152 | tf_op jit(solution)/shard_map/convert_element_type | solution.py:101
  34.0 0.4 convolution_bitcast_fusion.2
  34.5 20.4 %all_gather.7 = f32[32,2,8,256]{3,2,0,1:T(8,128)S(1)} all-gather(f32[2,2,8,256]{3,2,0,1:T(8,128)S(1)} %maximum_multiply_fusion), channel_id=1, replica_groups=mesh['grp'=2,'sub'=16] {'sub'}, dimensions={0}, use_global_device_ids=true | all-gather | bytes 557056 | tf_op jit(solution)/shard_map/all_gather | solution.py:109
  54.9 1.0 %fusion.8 = f32[32,12,2,256]{3,1,2,0:T(8,128)S(1)} fusion(f32[32,2,8,256]{3,2,0,1:T(8,128)S(1)} %all_gather.7, s32[32,8]{1,0:T(8,128)S(1)} %add_select_fusion), kind=kOutput, calls=%fused_computation.21 | convolution fusion | flops 18877440 | bytes 1311744 | tf_op jit(solution)/shard_map/spw,scpr->swcr/dot_general | solution.py:49
  55.8 0.5 copy.57
  56.7 0.3 convolution_bitcast_fusion.4
  57.0 2.9 %collective-permute-start.4 = (f32[4,2,256]{2,0,1:T(4,128)S(1)}, f32[4,2,256]{2,0,1:T(4,128)S(1)}, u32[]{:S(2)}, u32[]{:S(2)}) collective-permute-start(f32[4,2,256]{2,0,1:T(4,128)S(1)} %get-tuple-element.23), channel_id=1, source_target_pairs={{0,1},{1,2},{2,3},{3,4},{4,5},{5,6},{6,7},{7,8},{8,9},{9,10},{10,1... | collective-permute-start | bytes 24584 | tf_op jit(solution)/shard_map/ppermute | solution.py:14
  59.8 1.3 %convolution_bitcast_fusion = f32[2,2,2,512,256]{3,4,1,2,0:T(8,128)S(1)} fusion(bf16[1,2,2,512,512]{4,3,2,1,0:T(8,128)(2,1)S(1)} %copy-done, bf16[2,2,256,256]{2,3,1,0:T(8,128)(2,1)S(1)} %slice.170, bf16[2,2,256,256]{2,3,1,0:T(8,128)(2,1)S(1)} %fusion.7), kind=kOutput, calls=%fused_computation | convolution fusion | flops 1075838976 | bytes 7340032 | tf_op jit(solution)/shard_map/scik,sdkr->scdir/dot_general | solution.py:24
  61.6 4.0 %collective-permute-done.5 = f32[4,2,256]{2,0,1:T(4,128)S(1)} collective-permute-done((f32[4,2,256]{2,0,1:T(4,128)S(1)}, f32[4,2,256]{2,0,1:T(4,128)S(1)}, u32[]{:S(2)}, u32[]{:S(2)}) %collective-permute-start.5) | collective-permute-done | bytes 8224 | tf_op jit(solution)/shard_map/ppermute | solution.py:14
  65.8 1.9 %convolution_bitcast_fusion.1 = f32[2,2,2,512,256]{3,4,0,2,1:T(8,128)S(1)} fusion(f32[2,2,8,256,1]{3,2,1,0,4:T(8,128)S(1)} %convolution_bitcast_fusion.3, bf16[1,2,2,8,512]{4,3,2,1,0:T(8,128)(2,1)S(1)} %copy-done.1), kind=kOutput, calls=%fused_computation.1 | convolution fusion | flops 100663296 | bytes 4259840 | tf_op jit(solution)/shard_map/...cik,...dkr->...cdir/dot_general | solution.py:29
  67.7 0.5 fusion.3
  68.2 0.6 fusion
  68.8 1.3 %copy.63 = bf16[1,2,2,512,256]{4,3,2,1,0:T(8,128)(2,1)} copy(bf16[1,2,2,512,256]{3,4,1,2,0:T(8,128)(2,1)S(1)} %fusion) | data formatting | bytes 2097152 | tf_op jit(solution)/shard_map/convert_element_type | solution.py:121
  (34 shorter events, 1.3 us)
Async XLA Ops:
  0.0 59.8 %copy-start = (bf16[1,2,2,512,512]{4,3,2,1,0:T(8,128)(2,1)S(1)}, bf16[1,2,2,512,512]{4,3,2,1,0:T(8,128)(2,1)}, u32[]{:S(2)}) copy-start(bf16[1,2,2,512,512]{4,3,2,1,0:T(8,128)(2,1)} %param.7) | copy-start | bytes 6291460
  2.5 29.7 %collective-permute-start = (bf16[1,2,64,256]{2,3,1,0:T(8,128)(2,1)}, bf16[1,2,64,256]{2,3,1,0:T(8,128)(2,1)S(1)}, u32[]{:S(2)}, u32[]{:S(2)}) collective-permute-start(bf16[1,2,64,256]{2,3,1,0:T(8,128)(2,1)} %get-tuple-element.7), channel_id=1, source_target_pairs={{0,1},{1,2},{2,3},{3,4},{4,5},{5,6},{6,7},{7,8},{8,9},{9,10},{10,1... | collective-permute-start | bytes 196616 | tf_op jit(solution)/shard_map/ppermute | solution.py:14
  2.9 29.2 %collective-permute-start.1 = (bf16[1,2,64,256]{2,3,1,0:T(8,128)(2,1)}, bf16[1,2,64,256]{2,3,1,0:T(8,128)(2,1)}, u32[]{:S(2)}, u32[]{:S(2)}) collective-permute-start(bf16[1,2,64,256]{2,3,1,0:T(8,128)(2,1)} %get-tuple-element.8), channel_id=1, source_target_pairs={{0,15},{1,0},{2,1},{3,2},{4,3},{5,4},{6,5},{7,6},{8,7},{9,8},{10,9... | collective-permute-start | bytes 196616 | tf_op jit(solution)/shard_map/ppermute | solution.py:14
  4.0 28.1 %collective-permute-start.2 = (bf16[2,2,64,256]{2,3,1,0:T(8,128)(2,1)}, bf16[2,2,64,256]{2,3,1,0:T(8,128)(2,1)}, u32[]{:S(2)}, u32[]{:S(2)}) collective-permute-start(bf16[2,2,64,256]{2,3,1,0:T(8,128)(2,1)} %get-tuple-element.11), channel_id=1, source_target_pairs={{0,16},{1,17},{2,18},{3,19},{4,20},{5,21},{6,22},{7,23},{8,24},{9,... | collective-permute-start | bytes 393224 | tf_op jit(solution)/shard_map/ppermute | solution.py:20
  5.3 26.9 %collective-permute-start.3 = (bf16[2,2,64,256]{2,3,1,0:T(8,128)(2,1)}, bf16[2,2,64,256]{2,3,1,0:T(8,128)(2,1)}, u32[]{:S(2)}, u32[]{:S(2)}) collective-permute-start(bf16[2,2,64,256]{2,3,1,0:T(8,128)(2,1)} %get-tuple-element.12), channel_id=1, source_target_pairs={{16,0},{17,1},{18,2},{19,3},{20,4},{21,5},{22,6},{23,7},{24,8},{25... | collective-permute-start | bytes 393224 | tf_op jit(solution)/shard_map/ppermute | solution.py:20
  30.9 1.0 %copy-start.3 = (s32[32]{0:T(128)S(1)}, s32[32]{0:T(128)}, u32[]{:S(2)}) copy-start(s32[32]{0:T(128)} %iota_multiply_fusion) | copy-start | bytes 388
  30.9 1.1 %copy-start.4 = (s32[1,2]{1,0:T(1,128)S(1)}, s32[1,2]{1,0:T(1,128)}, u32[]{:S(2)}) copy-start(s32[1,2]{1,0:T(1,128)} %param.9) | copy-start | bytes 28
  32.1 1.8 %copy-start.1 = (bf16[1,2,2,8,512]{4,3,2,1,0:T(8,128)(2,1)S(1)}, bf16[1,2,2,8,512]{4,3,2,1,0:T(8,128)(2,1)}, u32[]{:S(2)}) copy-start(bf16[1,2,2,8,512]{4,3,2,1,0:T(8,128)(2,1)} %param.8) | copy-start | bytes 98308
  55.8 0.8 %copy-start.2 = (f32[1,2,8,128]{3,2,1,0:T(8,128)S(1)}, f32[1,2,8,128]{3,2,1,0:T(8,128)}, u32[]{:S(2)}) copy-start(f32[1,2,8,128]{3,2,1,0:T(8,128)} %param.11) | copy-start | bytes 24580
  57.0 4.6 %collective-permute-start.4 = (f32[4,2,256]{2,0,1:T(4,128)S(1)}, f32[4,2,256]{2,0,1:T(4,128)S(1)}, u32[]{:S(2)}, u32[]{:S(2)}) collective-permute-start(f32[4,2,256]{2,0,1:T(4,128)S(1)} %get-tuple-element.23), channel_id=1, source_target_pairs={{0,1},{1,2},{2,3},{3,4},{4,5},{5,6},{6,7},{7,8},{8,9},{9,10},{10,1... | collective-permute-start | bytes 24584 | tf_op jit(solution)/shard_map/ppermute | solution.py:14
  59.8 5.8 %collective-permute-start.5 = (f32[4,2,256]{2,0,1:T(4,128)S(1)}, f32[4,2,256]{2,0,1:T(4,128)S(1)}, u32[]{:S(2)}, u32[]{:S(2)}) collective-permute-start(f32[4,2,256]{2,0,1:T(4,128)S(1)} %get-tuple-element.24), channel_id=1, source_target_pairs={{0,15},{1,0},{2,1},{3,2},{4,3},{5,4},{6,5},{7,6},{8,7},{9,8},{10,9... | collective-permute-start | bytes 24584 | tf_op jit(solution)/shard_map/ppermute | solution.py:14
where the time goes:
time: 70.3 us; the launch traced here: 70.1 us
  blocking collectives  40 us (57%)
  starting transfers between devices  10.2 us (15%)
  local copies, waits for them, and re-layouts  5.44 us (8%)
  other arithmetic  5.16 us (7%)
  matrix products  4.95 us (7%)
  waiting for transfers between devices  4.05 us (6%)
    all_gather x1, blocking collectives, per_device(): lax.all_gather(primal, 'sub', axis=0, tiled=True)  20.4 us
    all_gather x1, blocking collectives, per_device(): lax.all_gather(mapped, 'sub', axis=0, tiled=True)  19.6 us
    ppermute x2, starting transfers between devices, shifted_2(): return lax.ppermute(block, axis, route)  6.66 us
    ppermute x4, waiting for transfers between devices, shifted(): return lax.ppermute(value, axis, pairs)  4.05 us
    ppermute x4, starting transfers between devices, shifted(): return lax.ppermute(value, axis, pairs)  3.53 us
    dot_general x1, matrix products, product_high(): jnp.einsum('...cik,...dkr->...cdir', matrix, vector, precision=lax.Precis...  1.86 us
    convert_element_type x1, other arithmetic, per_device(): shared.astype(jnp.bfloat16)  1.78 us
    unnamed x11, local copies, waits for them, and re-layouts  1.66 us
  transfers between devices with their start and end apart: 6, of which 1 were waited for; matrix products, arithmetic and copies ran while one was open for 6% of the time, Pallas kernels for 0%

commit v1 on v0

v1 whole, which is shorter than its diff:
```python
import functools

import jax
import jax.numpy as jnp
from jax import lax
from jax.experimental import pallas as pl
from jax.experimental.pallas import tpu as pltpu
from jax.sharding import PartitionSpec as P

IF = 64
CPS = 4
MESH = pl.DeviceIdType.MESH
F32 = jnp.float32
BF16 = jnp.bfloat16


def dot(a, b):
    return jnp.dot(a, b, preferred_element_type=F32)


def repeat(first, last, body):
    if last - first <= 8:
        for k in range(first, last):
            body(k)
    else:
        lax.fori_loop(first, last, lambda k, c: (body(k), c)[1], 0)


def split(x):
    high = x.astype(BF16)
    return high, (x - high.astype(F32)).astype(BF16)


def kernel(
    n, groups, resid, kinv, basis, counts, cmap, coarse, out,
    vals, kin, below, above, fprev, fnext, cprev, cnext, gather, wt, acc,
    load_sem, halo_send, halo_recv, ag_send, ag_recv,
):
    subs, _, order, width = vals.shape
    shared = 4 * IF
    rows_own, nc = coarse.shape[2], coarse.shape[3]
    rows_w = gather.shape[2]
    me = lax.axis_index("sub")
    grp = lax.axis_index("grp")
    nxt, prv = lax.rem(me + 1, n), lax.rem(me + n - 1, n)
    chips = n // 2
    chip, core = me // 2, lax.rem(me, 2)
    sib = chip * 2 + 1 - core
    has_below, has_above = grp > 0, grp < groups - 1

    barrier = pltpu.get_barrier_semaphore()

    def greet(k):
        pl.semaphore_signal(
            barrier, inc=1, device_id={"sub": lax.rem(me + k, n)}, device_id_type=MESH
        )

    @pl.when(has_above)
    def _():
        pl.semaphore_signal(barrier, inc=1, device_id={"grp": grp + 1}, device_id_type=MESH)

    @pl.when(has_below)
    def _():
        pl.semaphore_signal(barrier, inc=1, device_id={"grp": grp - 1}, device_id_type=MESH)

    if n <= 16:
        for k in range(1, n):
            greet(k)
    else:
        repeat(1, n, greet)

    load_vals = pltpu.make_async_copy(resid.at[0], vals, load_sem.at[0])
    load_kinv = pltpu.make_async_copy(kinv.at[0], kin, load_sem.at[1])
    load_vals.start()
    load_kinv.start()

    def push(i, src, dst, where):
        return pltpu.make_async_remote_copy(
            src_ref=src, dst_ref=dst, send_sem=halo_send.at[i], recv_sem=halo_recv.at[i],
            device_id=where, device_id_type=MESH,
        )

    to_next = push(0, resid.at[0, subs - 1, :, pl.ds(IF, IF)], fprev, {"sub": nxt})
    to_prev = push(1, resid.at[0, 0, :, pl.ds(0, IF)], fnext, {"sub": prv})
    to_above = push(2, resid.at[0, :, :, pl.ds(3 * IF, IF)], below, {"grp": grp + 1})
    to_below = push(3, resid.at[0, :, :, pl.ds(2 * IF, IF)], above, {"grp": grp - 1})
    c_next = push(4, coarse, cprev, {"sub": nxt})
    c_prev = push(5, coarse, cnext, {"sub": prv})

    pl.semaphore_wait(
        barrier, n - 1 + has_above.astype(jnp.int32) + has_below.astype(jnp.int32)
    )

    @pl.when(has_above)
    def _():
        to_above.start()

    @pl.when(has_below)
    def _():
        to_below.start()

    to_next.start()
    to_prev.start()
    c_next.start()
    c_prev.start()

    windowed = []
    for s in range(subs):
        relative = cmap[0, s : s + 1, :] - CPS * (me * subs + s) + CPS
        relative = jnp.where(relative < 0, relative + nc, relative)
        relative = jnp.where(relative >= nc, relative - nc, relative) + CPS * s
        pmax = relative.shape[1]
        spots = lax.broadcasted_iota(jnp.int32, (rows_w, pmax), 0)
        slots = lax.broadcasted_iota(jnp.int32, (rows_w, pmax), 1)
        hit = (spots == relative) & (slots < counts[:, s : s + 1])
        table = hit.astype(F32).astype(BF16)
        both = [dot(table, basis[0, s, c]) for c in range(2)]
        windowed.append(jnp.concatenate(both, axis=0))

    rows = lax.broadcasted_iota(jnp.int32, (nc, n * rows_w), 0)
    cols = lax.broadcasted_iota(jnp.int32, (nc, n * rows_w), 1)
    place = (cols // rows_w) * rows_own - CPS + lax.rem(cols, rows_w)
    place = jnp.where(place < 0, place + nc, place)
    place = jnp.where(place >= nc, place - nc, place)
    within = lax.rem(cols, rows_w) < rows_own + 2 * CPS
    pick = ((rows == place) & within).astype(F32).astype(BF16)

    load_vals.wait()
    load_kinv.wait()

    def combine(k_cols, real, imag):
        lhs = jnp.concatenate(k_cols, axis=1)
        rhs_real = jnp.concatenate([real, -imag], axis=0)
        rhs_imag = jnp.concatenate([imag, real], axis=0)
        return dot(lhs, rhs_real), dot(lhs, rhs_imag)

    def window_part(table, real, imag):
        high = table.astype(BF16)
        both_real, both_imag = dot(high, real), dot(high, imag)
        return (
            both_real[:rows_w] - both_imag[rows_w:],
            both_imag[:rows_w] + both_real[rows_w:],
        )

    w_real = jnp.zeros((rows_w, width), F32)
    w_imag = jnp.zeros((rows_w, width), F32)
    for s in range(subs):
        real, imag = vals[s, 0, shared:], vals[s, 1, shared:]
        part = window_part(windowed[s][:, shared:], real, imag)
        w_real, w_imag = w_real + part[0], w_imag + part[1]
        got = combine([kin[s, 0, :, shared:], kin[s, 1, :, shared:]], real, imag)
        acc[s, 0], acc[s, 1] = got

    to_next.wait_recv()
    to_prev.wait_recv()

    @pl.when(has_below)
    def _():
        to_above.wait_recv()

    @pl.when(has_above)
    def _():
        to_below.wait_recv()

    low = jnp.where(has_below, 0.5, 1.0).astype(F32)
    high = jnp.where(has_above, 0.5, 1.0).astype(F32)
    for s in range(subs):
        for c in range(2):
            own = [vals[s, c, IF * i : IF * (i + 1)].astype(F32) for i in range(4)]
            left = fprev[c] if s == 0 else vals[s - 1, c, IF : 2 * IF]
            right = fnext[c] if s == subs - 1 else vals[s + 1, c, 0:IF]
            zero = jnp.zeros((IF, width), F32)
            under = jnp.where(has_below, below[s, c].astype(F32), zero)
            over = jnp.where(has_above, above[s, c].astype(F32), zero)
            wt[s, c, 0:IF] = (0.5 * own[0] + 0.5 * left.astype(F32)).astype(BF16)
            wt[s, c, IF : 2 * IF] = (0.5 * own[1] + 0.5 * right.astype(F32)).astype(BF16)
            wt[s, c, 2 * IF : 3 * IF] = (low * own[2] + 0.5 * under).astype(BF16)
            wt[s, c, 3 * IF : 4 * IF] = (high * own[3] + 0.5 * over).astype(BF16)
        part = window_part(windowed[s][:, :shared], wt[s, 0], wt[s, 1])
        w_real, w_imag = w_real + part[0], w_imag + part[1]

    gather[me, 0] = w_real.astype(BF16)
    gather[me, 1] = w_imag.astype(BF16)

    def share(slot, where, i):
        return pltpu.make_async_remote_copy(
            src_ref=gather.at[slot], dst_ref=gather.at[slot],
            send_sem=ag_send.at[i], recv_sem=ag_recv.at[slot],
            device_id={"sub": where}, device_id_type=MESH,
        )

    def across(k):
        return share(me, lax.rem(chip + k, chips) * 2 + core, k)

    def source(k):
        return lax.rem(chip + chips - k, chips) * 2 + core

    def relay(k):
        return share(source(k), sib, chips + k)

    repeat(1, chips, lambda k: across(k).start())
    share(me, sib, 0).start()

    c_next.wait_recv()
    c_prev.wait_recv()
    pieces = []
    for c in range(2):
        parts = [cprev[0, c, rows_own - CPS :], coarse[0, c], cnext[0, c, :CPS]]
        extra = rows_w - rows_own - 2 * CPS
        if extra:
            parts.append(jnp.zeros((extra, nc), F32))
        pieces.extend(split(jnp.concatenate(parts, axis=0)))
    coarse_ext = dot(jnp.concatenate(pieces, axis=0), pick).astype(BF16)
    columns = [w.astype(BF16).T for w in windowed]

    def forward(k):
        share(source(k), sib, k).wait_recv()
        relay(k).start()

    for s in range(subs):
        got = combine([kin[s, 0, :, :shared], kin[s, 1, :, :shared]], wt[s, 0], wt[s, 1])
        acc[s, 0] += got[0]
        acc[s, 1] += got[1]

    repeat(1, chips, forward)
    repeat(0, chips, lambda k: share(lax.rem(chip + k, chips) * 2 + 1 - core, sib, 0).wait_recv())

    all_real = gather[:, 0].reshape(n * rows_w, width)
    all_imag = gather[:, 1].reshape(n * rows_w, width)
    by_real, by_imag = dot(coarse_ext, all_real), dot(coarse_ext, all_imag)

    def whole(x, i):
        return x[2 * i * rows_w : (2 * i + 1) * rows_w] + x[(2 * i + 1) * rows_w : (2 * i + 2) * rows_w]

    solved_real = whole(by_real, 0) - whole(by_imag, 1)
    solved_imag = whole(by_imag, 0) + whole(by_real, 1)
    real_high, real_low = split(solved_real)
    imag_high, imag_low = split(solved_imag)
    rhs_real = jnp.concatenate([real_high, -imag_high, real_low, -imag_low], axis=0)
    rhs_imag = jnp.concatenate([imag_high, real_high, imag_low, real_low], axis=0)
    for s in range(subs):
        lhs = jnp.concatenate([columns[s], columns[s]], axis=1)
        out[0, s, 0] = (acc[s, 0] + dot(lhs, rhs_real)).astype(BF16)
        out[0, s, 1] = (acc[s, 1] + dot(lhs, rhs_imag)).astype(BF16)

    to_next.wait_send()
    to_prev.wait_send()

    @pl.when(has_above)
    def _():
        to_above.wait_send()

    @pl.when(has_below)
    def _():
        to_below.wait_send()

    c_next.wait_send()
    c_prev.wait_send()
    share(me, sib, 0).wait_send()
    repeat(1, chips, lambda k: across(k).wait_send())
    repeat(1, chips, lambda k: relay(k).wait_send())


def per_device(n, groups, resid, kinv, basis, counts, coarse_map, coarse_inv):
    _, subs, _, order, width = resid.shape
    rows_w = -(-(CPS * (subs + 2)) // 16) * 16
    vmem = pl.BlockSpec(memory_space=pltpu.VMEM)
    hbm = pl.BlockSpec(memory_space=pl.ANY)
    dma = pltpu.SemaphoreType.DMA
    return pl.pallas_call(
        functools.partial(kernel, n, groups),
        out_shape=jax.ShapeDtypeStruct(resid.shape, BF16),
        in_specs=[hbm, hbm, vmem, vmem, vmem, vmem],
        out_specs=vmem,
        scratch_shapes=[
            pltpu.VMEM(resid.shape[1:], BF16),
            pltpu.VMEM(kinv.shape[1:], BF16),
            pltpu.VMEM((subs, 2, IF, width), BF16),
            pltpu.VMEM((subs, 2, IF, width), BF16),
            pltpu.VMEM((2, IF, width), BF16),
            pltpu.VMEM((2, IF, width), BF16),
            pltpu.VMEM(coarse_inv.shape, F32),
            pltpu.VMEM(coarse_inv.shape, F32),
            pltpu.VMEM((n, 2, rows_w, width), BF16),
            pltpu.VMEM((subs, 2, 4 * IF, width), BF16),
            pltpu.VMEM((subs, 2, order, width), F32),
            dma((2,)), dma((6,)), dma((6,)), dma((n,)), dma((n,)),
        ],
        compiler_params=pltpu.CompilerParams(collective_id=0, has_side_effects=True),
    )(resid, kinv, basis, counts, coarse_map, coarse_inv)


def solution(mesh):
    return jax.shard_map(
        functools.partial(per_device, mesh.shape["sub"], mesh.shape["grp"]),
        mesh=mesh,
        in_specs=(
            P("grp", "sub", None, None, None),
            P("grp", "sub", None, None, None),
            P("grp", "sub", None, None, None),
            P("grp", "sub"),
            P("grp", "sub", None),
            P("grp", None, "sub", None),
        ),
        out_specs=P("grp", "sub", None, None, None),
        check_vma=False,
    )
```

time: 70.3 us -> 21.4 us (0.30)
  the two profiles are of different devices: /device:TPU:31 before, /device:TPU:1 now
where the time goes in v1:
time: 21.4 us; the launch traced here: 21.2 us
  Pallas kernels  18.9 us (88%)
  local copies, waits for them, and re-layouts  2.26 us (11%)
    pallas_call x1, Pallas kernels, per_device(): pl.pallas_call(functools.partial(kernel, n, groups), out_shape=jax.ShapeD...  18.9 us
    unnamed x1, local copies, waits for them, and re-layouts  2.26 us

profile of v1, /device:TPU:1, one launch (start us, length us, event | category | flops | bytes accessed | tf_op | source)
XLA Modules:
  0.0 21.2 jit_solution(11521593749915640748)
XLA Ops:
  0.0 18.9 %shard_map.64 = bf16[1,2,2,512,256]{4,3,2,1,0:T(8,128)(2,1)} custom-call(bf16[1,2,2,512,256]{4,3,2,1,0:T(8,128)(2,1)} %resid.1, bf16[1,2,2,512,512]{4,3,2,1,0:T(8,128)(2,1)} %kinv.1, bf16[1,2,2,8,512]{4,3,2,1,0:T(8,128)(2,1)} %basis.1, s32[1,2]{1,0:T(1,128)} %counts.1, s32[1,2,8]{2,1,0:T(2,128)} %cmap.1, f32[1,2,8,128]{3,2,1,0:T(8,128)} %coarse.1), custom_call_target="tpu_custom_call" | custom-call | tf_op jit(solution)/shard_map/pallas_call | solution.py:270
  18.9 2.3 %copy.8 = bf16[1,2,2,512,256]{4,3,2,1,0:T(8,128)(2,1)} copy(bf16[1,2,2,512,256]{4,3,2,1,0:T(8,128)(2,1)} %shard_map.64) | data formatting | bytes 2097152

commit v2 on v1

--- a/solution.py
+++ b/solution.py
@@ -32,8 +32,8 @@
 
 
 def kernel(
-    n, groups, resid, kinv, basis, counts, cmap, coarse, out,
-    vals, kin, below, above, fprev, fnext, cprev, cnext, gather, wt, acc,
+    n, groups, resid, kinv, basis_hbm, counts_hbm, cmap_hbm, coarse_hbm, out,
+    basis, counts, cmap, coarse, vals, kin, below, above, fprev, fnext, cprev, cnext, gather, wt, acc,
     load_sem, halo_send, halo_recv, ag_send, ag_recv,
 ):
     subs, _, order, width = vals.shape
@@ -63,14 +63,26 @@
     def _():
         pl.semaphore_signal(barrier, inc=1, device_id={"grp": grp - 1}, device_id_type=MESH)
 
-    if n <= 16:
-        for k in range(1, n):
-            greet(k)
-    else:
-        repeat(1, n, greet)
+    def greet_chip(k):
+        pl.semaphore_signal(
+            barrier, inc=1, device_id={"sub": lax.rem(chip + k, chips) * 2 + core}, device_id_type=MESH
+        )
+
+    repeat(1, chips, greet_chip)
+    pl.semaphore_signal(barrier, inc=1, device_id={"sub": sib}, device_id_type=MESH)
+    beyond = jnp.where(core == 1, nxt, prv)
+    pl.semaphore_signal(barrier, inc=1, device_id={"sub": beyond}, device_id_type=MESH)
 
     load_vals = pltpu.make_async_copy(resid.at[0], vals, load_sem.at[0])
     load_kinv = pltpu.make_async_copy(kinv.at[0], kin, load_sem.at[1])
+    small = [
+        pltpu.make_async_copy(src, dst, load_sem.at[2 + i])
+        for i, (src, dst) in enumerate(
+            [(coarse_hbm, coarse), (cmap_hbm, cmap), (counts_hbm, counts), (basis_hbm, basis)]
+        )
+    ]
+    for load in small:
+        load.start()
     load_vals.start()
     load_kinv.start()
 
@@ -87,8 +99,10 @@
     c_next = push(4, coarse, cprev, {"sub": nxt})
     c_prev = push(5, coarse, cnext, {"sub": prv})
 
+    for load in small:
+        load.wait()
     pl.semaphore_wait(
-        barrier, n - 1 + has_above.astype(jnp.int32) + has_below.astype(jnp.int32)
+        barrier, chips + 1 + has_above.astype(jnp.int32) + has_below.astype(jnp.int32)
     )
 
     @pl.when(has_above)
@@ -265,14 +279,18 @@
     _, subs, _, order, width = resid.shape
     rows_w = -(-(CPS * (subs + 2)) // 16) * 16
     vmem = pl.BlockSpec(memory_space=pltpu.VMEM)
-    hbm = pl.BlockSpec(memory_space=pl.ANY)
+    hbm = pl.BlockSpec(memory_space=pltpu.HBM)
     dma = pltpu.SemaphoreType.DMA
     return pl.pallas_call(
         functools.partial(kernel, n, groups),
-        out_shape=jax.ShapeDtypeStruct(resid.shape, BF16),
-        in_specs=[hbm, hbm, vmem, vmem, vmem, vmem],
+        out_shape=pltpu.VMEM(resid.shape, BF16),
+        in_specs=[hbm] * 6,
         out_specs=vmem,
         scratch_shapes=[
+            pltpu.VMEM(basis.shape, BF16),
+            pltpu.VMEM(counts.shape, jnp.int32),
+            pltpu.VMEM(coarse_map.shape, jnp.int32),
+            pltpu.VMEM(coarse_inv.shape, F32),
             pltpu.VMEM(resid.shape[1:], BF16),
             pltpu.VMEM(kinv.shape[1:], BF16),
             pltpu.VMEM((subs, 2, IF, width), BF16),
@@ -284,7 +302,7 @@
             pltpu.VMEM((n, 2, rows_w, width), BF16),
             pltpu.VMEM((subs, 2, 4 * IF, width), BF16),
             pltpu.VMEM((subs, 2, order, width), F32),
-            dma((2,)), dma((6,)), dma((6,)), dma((n,)), dma((n,)),
+            dma((6,)), dma((6,)), dma((6,)), dma((n,)), dma((n,)),
         ],
         compiler_params=pltpu.CompilerParams(collective_id=0, has_side_effects=True),
     )(resid, kinv, basis, counts, coarse_map, coarse_inv)

time: 21.4 us -> 18.3 us (0.86)
  Pallas kernels: 18.9 us -> 17.2 us
  local copies, waits for them, and re-layouts: 2.26 us -> 0.97 us
    pallas_call x1, Pallas kernels: 18.9 us -> 17.2 us  [per_device(): pl.pallas_call(functools.partial(kernel, n, groups), out_shape=pltpu.VMEM...]
    unnamed x1, local copies, waits for them, and re-layouts: 2.26 us -> 0.97 us
where the time goes in v2:
time: 18.3 us; the launch traced here: 18.1 us
  Pallas kernels  17.2 us (94%)
  local copies, waits for them, and re-layouts  0.97 us (5%)
    pallas_call x1, Pallas kernels, per_device(): pl.pallas_call(functools.partial(kernel, n, groups), out_shape=pltpu.VMEM...  17.2 us
    unnamed x1, local copies, waits for them, and re-layouts  0.97 us

profile of v2, /device:TPU:1, one launch (start us, length us, event | category | flops | bytes accessed | tf_op | source)
XLA Modules:
  0.0 18.1 jit_solution(2419218500886458620)
XLA Ops:
  0.0 17.2 %shard_map.64 = bf16[1,2,2,512,256]{4,3,2,1,0:T(8,128)(2,1)S(1)} custom-call(bf16[1,2,2,512,256]{4,3,2,1,0:T(8,128)(2,1)} %resid.1, bf16[1,2,2,512,512]{4,3,2,1,0:T(8,128)(2,1)} %kinv.1, bf16[1,2,2,8,512]{4,3,2,1,0:T(8,128)(2,1)} %basis_hbm.1, s32[1,2]{1,0:T(1,128)} %counts_hbm.1, s32[1,2,8]{2,1,0:T(2,128)} %cmap_hbm.1, f32[1,2,8,128]{3,2,1,0:T(8,128)} %coarse_hbm.1), custom_call_target="tpu_custom_call" | custom-call | tf_op jit(solution)/shard_map/pallas_call | solution.py:284
  17.2 1.0 %copy.8 = bf16[1,2,2,512,256]{4,3,2,1,0:T(8,128)(2,1)} copy(bf16[1,2,2,512,256]{4,3,2,1,0:T(8,128)(2,1)S(1)} %shard_map.64) | data formatting | bytes 2097152
